TPU v7x, 32 devices: a whole 2x2x4 slice. The times are simulated.
32 devices in a mesh: rep: 4 (over x, core), fsdp: 2 (over y), seq: 4 (over z).
Axes of the slice: x: 2, y: 2, z: 4, core: 2. Of those that a mesh axis runs over, the one named last changes fastest.
Arguments:
- tokens: bfloat16 [8, 512, 1024], P(('rep', 'fsdp'), 'seq'), may hold values from -6 to 6
- conditioning: bfloat16 [8, 1024], P(('rep', 'fsdp')), may hold values from -6 to 6
- cotangent: bfloat16 [8, 512, 1024], P(('rep', 'fsdp'), 'seq'), may hold values from -6 to 6
- ada_weight: bfloat16 [1024, 6144], P('fsdp'), may hold values from -0.1875 to 0.1875
- ada_bias: bfloat16 [6144], P('fsdp'), may hold values from -3 to 3
- qkv_weight: bfloat16 [1024, 3072], P('fsdp'), may hold values from -0.1875 to 0.1875
- qv_bias: bfloat16 [2048], P('fsdp'), may hold values from -3 to 3
- proj_weight: bfloat16 [1024, 1024], P('fsdp'), may hold values from -1 to 1
- proj_bias: bfloat16 [1024], P('fsdp'), may hold values from -3 to 3
- fc1_weight: bfloat16 [1024, 4096], P('fsdp'), may hold values from -0.1875 to 0.1875
- fc1_bias: bfloat16 [4096], P('fsdp'), may hold values from -3 to 3
- fc2_weight: bfloat16 [4096, 1024], P('fsdp'), may hold values from -0.09375 to 0.09375
- fc2_bias: bfloat16 [1024], P('fsdp'), may hold values from -3 to 3
Outputs:
- output: bfloat16 [8, 512, 1024], P(('rep', 'fsdp'), 'seq')
- tokens_grad: float32 [8, 512, 1024], P(('rep', 'fsdp'), 'seq')
- cond_grad: float32 [8, 1024], P(('rep', 'fsdp'))
- ada_weight_grad: float32 [1024, 6144], P('fsdp')
- ada_bias_grad: float32 [6144], P('fsdp')
- qkv_weight_grad: float32 [1024, 3072], P('fsdp')
- qv_bias_grad: float32 [2048], P('fsdp')
- proj_weight_grad: float32 [1024, 1024], P('fsdp')
- proj_bias_grad: float32 [1024], P('fsdp')
- fc1_weight_grad: float32 [1024, 4096], P('fsdp')
- fc1_bias_grad: float32 [4096], P('fsdp')
- fc2_weight_grad: float32 [4096, 1024], P('fsdp')
- fc2_bias_grad: float32 [1024], P('fsdp')
All inputs are finite; a program needn't handle non-finite values.
Results may differ from a plain program's by a relative error of at most 0.012.
The roundings to bfloat16 on the way count: a program that leaves them out, or rounds other values in their place, can miss the bound.
Values may be sent and summed in bfloat16 or wider, within the bound.
No kernel may reach another device: no remote copies, remote signals or barrier semaphores. Data moves between devices by JAX's collectives and lax.ppermute only.
A program may use at most 256 MiB of HBM per device.

v0:
```python
import jax
import jax.numpy as jnp
from jax import lax
from jax.sharding import PartitionSpec as P

HEADS = 16
HEAD_DIM = 64
EPSILON = 1e-06
TANH_ROOT = 0.7978845608028654
CUBIC_COEF = 0.044715


def product(left_op, right_op):
    return jnp.dot(left_op, right_op, preferred_element_type=jnp.float32)


def product_tn(left_op, right_op):
    return lax.dot_general(
        left_op, right_op, (((0,), (0,)), ((), ())), preferred_element_type=jnp.float32
    )


def product_nt(left_op, right_op):
    return lax.dot_general(
        left_op, right_op, (((1,), (1,)), ((), ())), preferred_element_type=jnp.float32
    )


def gelu_parts(pre_act):
    tanh_val = jnp.tanh(TANH_ROOT * (pre_act + CUBIC_COEF * pre_act * pre_act * pre_act))
    gelu_val = 0.5 * pre_act * (1.0 + tanh_val)
    gelu_slope = 0.5 * (1.0 + tanh_val) + 0.5 * pre_act * (
        1.0 - tanh_val * tanh_val
    ) * TANH_ROOT * (1.0 + 3.0 * CUBIC_COEF * pre_act * pre_act)
    return (gelu_val, gelu_slope)


def layer_norm(values):
    center = values - jnp.mean(values, axis=-1, keepdims=True)
    inv_std = lax.rsqrt(jnp.mean(center * center, axis=-1, keepdims=True) + EPSILON)
    return (center * inv_std, inv_std)


def norm_back(normed, inv_std, grad_in):
    return inv_std * (
        grad_in
        - jnp.mean(grad_in, axis=-1, keepdims=True)
        - normed * jnp.mean(grad_in * normed, axis=-1, keepdims=True)
    )


def silu_slope(condition):
    sigmoid_c = jax.nn.sigmoid(condition)
    return sigmoid_c * (1.0 + condition * (1.0 - sigmoid_c))


def split_heads(values):
    return values.reshape(values.shape[0], HEADS, values.shape[1] // HEADS)


def attend(query_rows, key_rows, value_rows):
    score_scale = HEAD_DIM ** (-0.5)
    scores = (
        jnp.einsum(
            "qhd,khd->hqk",
            split_heads(query_rows),
            split_heads(key_rows),
            preferred_element_type=jnp.float32,
        )
        * score_scale
    )
    row_max = jnp.max(scores, axis=-1, keepdims=True)
    exponent = jnp.exp(scores - row_max)
    row_total = jnp.sum(exponent, axis=-1, keepdims=True)
    attn_probs = (exponent / row_total).astype(jnp.bfloat16)
    attended = jnp.einsum(
        "hqk,khd->qhd", attn_probs, split_heads(value_rows), preferred_element_type=jnp.float32
    )
    attended = attended.reshape(query_rows.shape[0], query_rows.shape[1]).astype(jnp.bfloat16)
    return (attended, row_max + jnp.log(row_total))


def attend_back(query_rows, key_rows, value_rows, log_total, attended_grad):
    score_scale = HEAD_DIM ** (-0.5)
    query_heads, key_heads, value_heads = (
        split_heads(query_rows),
        split_heads(key_rows),
        split_heads(value_rows),
    )
    grad_heads = split_heads(attended_grad)
    scores = (
        jnp.einsum("qhd,khd->hqk", query_heads, key_heads, preferred_element_type=jnp.float32)
        * score_scale
    )
    probs_again = jnp.exp(scores - log_total)
    value_grad = jnp.einsum(
        "hqk,qhd->khd",
        probs_again.astype(jnp.bfloat16),
        grad_heads,
        preferred_element_type=jnp.float32,
    )
    prob_grad = jnp.einsum(
        "qhd,khd->hqk", grad_heads, value_heads, preferred_element_type=jnp.float32
    )
    row_delta = jnp.sum(probs_again * prob_grad, axis=-1, keepdims=True)
    score_grad = (probs_again * (prob_grad - row_delta) * score_scale).astype(jnp.bfloat16)
    query_grad = jnp.einsum(
        "hqk,khd->qhd", score_grad, key_heads, preferred_element_type=jnp.float32
    )
    key_grad = jnp.einsum(
        "hqk,qhd->khd", score_grad, query_heads, preferred_element_type=jnp.float32
    )
    model_width = query_rows.shape[1]
    return (
        query_grad.reshape(query_rows.shape[0], model_width),
        key_grad.reshape(key_rows.shape[0], model_width),
        value_grad.reshape(key_rows.shape[0], model_width),
    )


def local(
    tokens,
    conditioning,
    cotangent,
    ada_weight,
    ada_bias,
    qkv_weight,
    qv_bias,
    proj_weight,
    proj_bias,
    fc1_weight,
    fc1_bias,
    fc2_weight,
    fc2_bias,
):
    local_tokens = tokens[0]
    model_width = local_tokens.shape[1]
    cond_f = conditioning.astype(jnp.float32)
    silu_cond = jax.nn.silu(cond_f).astype(jnp.bfloat16)
    (
        qkv_full,
        qv_full,
        proj_full,
        projb_full,
        fc1_full,
        fc1b_full,
        fc2_full,
        fc2b_full,
        adab_full,
    ) = (
        lax.all_gather(qkv_weight, "fsdp", axis=0, tiled=True),
        lax.all_gather(qv_bias, "fsdp", axis=0, tiled=True),
        lax.all_gather(proj_weight, "fsdp", axis=0, tiled=True),
        lax.all_gather(proj_bias, "fsdp", axis=0, tiled=True),
        lax.all_gather(fc1_weight, "fsdp", axis=0, tiled=True),
        lax.all_gather(fc1_bias, "fsdp", axis=0, tiled=True),
        lax.all_gather(fc2_weight, "fsdp", axis=0, tiled=True),
        lax.all_gather(fc2_bias, "fsdp", axis=0, tiled=True),
        lax.all_gather(ada_bias, "fsdp", axis=0, tiled=True),
    )
    share = ada_weight.shape[0]
    groups = lax.axis_size("fsdp")
    cond_all = lax.all_gather(silu_cond, "fsdp", axis=0, tiled=True)
    own_cols = lax.dynamic_slice_in_dim(cond_all, lax.axis_index("fsdp") * share, share, 1)
    mods = lax.psum_scatter(product(own_cols, ada_weight), "fsdp", scatter_dimension=0, tiled=True)[
        0
    ]
    mods = mods + adab_full.astype(jnp.float32)
    shift_attn, scale_attn, gate_attn, shift_mlp, scale_mlp, gate_mlp = jnp.split(mods, 6)
    tokens_f = local_tokens.astype(jnp.float32)
    normed1, inv_std1 = layer_norm(tokens_f)
    hidden1 = (normed1 * (1.0 + scale_attn) + shift_attn).astype(jnp.bfloat16)
    qkv_rows = product(hidden1, qkv_full)
    qv_float = qv_full.astype(jnp.float32)
    query_rows = (qkv_rows[:, :model_width] + qv_float[:model_width]).astype(jnp.bfloat16)
    key_rows = qkv_rows[:, model_width : 2 * model_width].astype(jnp.bfloat16)
    value_rows = (qkv_rows[:, 2 * model_width :] + qv_float[model_width:]).astype(jnp.bfloat16)
    key_all, value_all = (
        lax.all_gather(key_rows, "seq", axis=0, tiled=True),
        lax.all_gather(value_rows, "seq", axis=0, tiled=True),
    )
    attended, log_total = attend(query_rows, key_all, value_all)
    branch = product(attended, proj_full) + projb_full.astype(jnp.float32)
    middle = tokens_f + gate_attn * branch
    normed2, inv_std2 = layer_norm(middle)
    hidden2 = (normed2 * (1.0 + scale_mlp) + shift_mlp).astype(jnp.bfloat16)
    pre_act = product(hidden2, fc1_full) + fc1b_full.astype(jnp.float32)
    gelu_val, gelu_slope = gelu_parts(pre_act)
    active = gelu_val.astype(jnp.bfloat16)
    mlp_out = product(active, fc2_full) + fc2b_full.astype(jnp.float32)
    output = (middle + gate_mlp * mlp_out).astype(jnp.bfloat16)
    qkv_back, proj_back, fc1_back, fc2_back = (
        lax.all_gather(qkv_weight, "fsdp", axis=0, tiled=True),
        lax.all_gather(proj_weight, "fsdp", axis=0, tiled=True),
        lax.all_gather(fc1_weight, "fsdp", axis=0, tiled=True),
        lax.all_gather(fc2_weight, "fsdp", axis=0, tiled=True),
    )
    cot_f = cotangent[0].astype(jnp.float32)
    mlp_grad = (gate_mlp * cot_f).astype(jnp.bfloat16)
    gate_mlp_grad = jnp.sum(cot_f * mlp_out, axis=0)
    pre_grad = (product_nt(mlp_grad, fc2_back) * gelu_slope).astype(jnp.bfloat16)
    fc1_bias_grad = jnp.sum(pre_grad.astype(jnp.float32), axis=0)
    hidden2_grad = product_nt(pre_grad, fc1_back)
    shift_mlp_grad = jnp.sum(hidden2_grad, axis=0)
    scale_mlp_grad = jnp.sum(hidden2_grad * normed2, axis=0)
    middle_grad = cot_f + norm_back(normed2, inv_std2, hidden2_grad * (1.0 + scale_mlp))
    gate_attn_grad = jnp.sum(middle_grad * branch, axis=0)
    branch_grad = (gate_attn * middle_grad).astype(jnp.bfloat16)
    attended_grad = product_nt(branch_grad, proj_back).astype(jnp.bfloat16)
    query_grad, key_part, value_part = attend_back(
        query_rows, key_all, value_all, log_total, attended_grad
    )
    key_grad, value_grad = (
        lax.psum_scatter(key_part, "seq", scatter_dimension=0, tiled=True),
        lax.psum_scatter(value_part, "seq", scatter_dimension=0, tiled=True),
    )
    query_b = query_grad.astype(jnp.bfloat16)
    value_b = value_grad.astype(jnp.bfloat16)
    qkv_grad = jnp.concatenate([query_b, key_grad.astype(jnp.bfloat16), value_b], axis=1)
    qv_bias_grad = jnp.concatenate(
        [jnp.sum(query_b.astype(jnp.float32), axis=0), jnp.sum(value_b.astype(jnp.float32), axis=0)]
    )
    hidden1_grad = product_nt(qkv_grad, qkv_back)
    shift_attn_grad = jnp.sum(hidden1_grad, axis=0)
    scale_attn_grad = jnp.sum(hidden1_grad * normed1, axis=0)
    tokens_grad = middle_grad + norm_back(normed1, inv_std1, hidden1_grad * (1.0 + scale_attn))
    mods_grad = jnp.concatenate(
        [
            shift_attn_grad,
            scale_attn_grad,
            gate_attn_grad,
            shift_mlp_grad,
            scale_mlp_grad,
            gate_mlp_grad,
        ]
    )
    proj_bias_grad = jnp.sum(branch_grad.astype(jnp.float32), axis=0)
    fc2_bias_grad = jnp.sum(mlp_grad.astype(jnp.float32), axis=0)
    hidden1_cols, hidden2_cols, active_cols, attended_cols = (
        lax.all_to_all(hidden1, "fsdp", split_axis=1, concat_axis=0, tiled=True),
        lax.all_to_all(hidden2, "fsdp", split_axis=1, concat_axis=0, tiled=True),
        lax.all_to_all(active, "fsdp", split_axis=1, concat_axis=0, tiled=True),
        lax.all_to_all(attended, "fsdp", split_axis=1, concat_axis=0, tiled=True),
    )
    qkv_all, pre_all, mlp_all, branch_all = (
        lax.all_gather(qkv_grad, "fsdp", axis=0, tiled=True),
        lax.all_gather(pre_grad, "fsdp", axis=0, tiled=True),
        lax.all_gather(mlp_grad, "fsdp", axis=0, tiled=True),
        lax.all_gather(branch_grad, "fsdp", axis=0, tiled=True),
    )
    qkv_shard = product_tn(hidden1_cols, qkv_all)
    fc1_shard = product_tn(hidden2_cols, pre_all)
    fc2_shard = product_tn(active_cols, mlp_all)
    proj_shard = product_tn(attended_cols, branch_all)
    qv_shard, projb_shard, fc1b_shard, fc2b_shard, adab_shard = (
        lax.psum_scatter(qv_bias_grad, "fsdp", scatter_dimension=0, tiled=True),
        lax.psum_scatter(proj_bias_grad, "fsdp", scatter_dimension=0, tiled=True),
        lax.psum_scatter(fc1_bias_grad, "fsdp", scatter_dimension=0, tiled=True),
        lax.psum_scatter(fc2_bias_grad, "fsdp", scatter_dimension=0, tiled=True),
        lax.psum_scatter(mods_grad, "fsdp", scatter_dimension=0, tiled=True),
    )
    mod_rows = lax.all_gather(mods_grad[None, :], ("fsdp", "seq"), axis=0, tiled=True)
    stacked = mod_rows.reshape(groups, mod_rows.shape[0] // groups, mod_rows.shape[1])
    own_seq = lax.dynamic_index_in_dim(stacked, lax.axis_index("seq"), 1, keepdims=False)
    ada_shard = lax.dot_general(
        own_cols.astype(jnp.float32),
        own_seq,
        (((0,), (0,)), ((), ())),
        precision=lax.Precision.HIGHEST,
    )
    cond_part = lax.dot_general(
        jnp.sum(stacked, axis=1),
        ada_weight.astype(jnp.float32),
        (((1,), (1,)), ((), ())),
        precision=lax.Precision.HIGHEST,
    )
    cond_sum = lax.all_to_all(cond_part, "fsdp", split_axis=0, concat_axis=1, tiled=True)
    cond_grad = cond_sum * silu_slope(cond_f)
    sums = lax.psum(
        (
            ada_shard,
            adab_shard,
            qkv_shard,
            qv_shard,
            proj_shard,
            projb_shard,
            fc1_shard,
            fc1b_shard,
            fc2_shard,
            fc2b_shard,
        ),
        ("rep", "seq"),
    )
    return (
        output[None],
        tokens_grad[None],
        cond_grad,
        sums[0],
        sums[1],
        sums[2],
        sums[3],
        sums[4],
        sums[5],
        sums[6],
        sums[7],
        sums[8],
        sums[9],
    )


def solution(mesh):
    in_specs = (
        P(("rep", "fsdp"), "seq", None),
        P(("rep", "fsdp"), None),
        P(("rep", "fsdp"), "seq", None),
        P("fsdp", None),
        P("fsdp"),
        P("fsdp", None),
        P("fsdp"),
        P("fsdp", None),
        P("fsdp"),
        P("fsdp", None),
        P("fsdp"),
        P("fsdp", None),
        P("fsdp"),
    )
    out_specs = (
        P(("rep", "fsdp"), "seq", None),
        P(("rep", "fsdp"), "seq", None),
        P(("rep", "fsdp"), None),
        P("fsdp", None),
        P("fsdp"),
        P("fsdp", None),
        P("fsdp"),
        P("fsdp", None),
        P("fsdp"),
        P("fsdp", None),
        P("fsdp"),
        P("fsdp", None),
        P("fsdp"),
    )
    return jax.shard_map(local, mesh=mesh, in_specs=in_specs, out_specs=out_specs, check_vma=False)
```

profile of v0, /device:TPU:0, one launch (start us, length us, event | category | flops | bytes accessed | tf_op | source)
XLA Modules:
  0.0 1255.6 jit_solution(5859581527247387863)
XLA Ops:
  28.7 10.4 all-reduce
  40.2 53.5 %all-gather.13.cloned.1.call-done = bf16[1024,3072]{1,0:T(8,128)(2,1)} async-done(((bf16[512,3072]{1,0:T(8,128)(2,1)}), bf16[1024,3072]{1,0:T(8,128)(2,1)}) %all-gather.13.cloned.1.call-update) | async-done | bytes 6291472 | tf_op jit(solution)/shard_map/all_gather | solution.py:151
  115.0 11.7 all-gather.15.cloned.1.call-done
  128.1 28.0 %all-gather.17.cloned.1.call-done = bf16[512,1024]{1,0:T(8,128)(2,1)} async-done(((bf16[128,1024]{1,0:T(8,128)(2,1)}), bf16[512,1024]{1,0:T(8,128)(2,1)}) %all-gather.17.cloned.1.call-update) | async-done | bytes 1048592 | tf_op jit(solution)/shard_map/all_gather | solution.py:179
  162.7 27.3 %all-gather.19.cloned.1.call-done = bf16[1024,1024]{1,0:T(8,128)(2,1)} async-done(((bf16[512,1024]{1,0:T(8,128)(2,1)}), bf16[1024,1024]{1,0:T(8,128)(2,1)}) %all-gather.19.cloned.1.call-update) | async-done | bytes 2097168 | tf_op jit(solution)/shard_map/all_gather | solution.py:153
  194.1 101.3 %all-gather.21.cloned.1.call-done = bf16[1024,4096]{1,0:T(8,128)(2,1)} async-done(((bf16[512,4096]{1,0:T(8,128)(2,1)}), bf16[1024,4096]{1,0:T(8,128)(2,1)}) %all-gather.21.cloned.1.call-update) | async-done | bytes 8388624 | tf_op jit(solution)/shard_map/all_gather | solution.py:155
  295.5 6.7 multiply_convert_fusion.1
  302.1 98.7 %all-gather.23.cloned.1.call-done = bf16[4096,1024]{1,0:T(8,128)(2,1)} async-done(((bf16[2048,1024]{1,0:T(8,128)(2,1)}), bf16[4096,1024]{1,0:T(8,128)(2,1)}) %all-gather.23.cloned.1.call-update) | async-done | bytes 8388624 | tf_op jit(solution)/shard_map/all_gather | solution.py:157
  400.9 8.5 convert_reduce_fusion
  409.6 6.9 multiply_reduce_fusion.2
  428.6 18.3 %fusion.8 = f32[16,64,512]{2,1,0:T(8,128)} fusion(bf16[128,16,64]{0,2,1:T(8,128)(2,1)S(1)} %bitcast.135, f32[16,128,512]{2,1,0:T(8,128)} %fusion.73, f32[16,128,512]{2,1,0:T(8,128)} %copy-done, f32[16,128]{1,0:T(8,128)S(1)} %log_add_fusion), kind=kOutput, calls=%fused_computation.15 | convolution fusion | flops 143657472 | bytes 10756096 | tf_op jit(solution)/shard_map/hqk,qhd->khd/dot_general | solution.py:110
  448.2 8.5 all_gather.71
  466.8 8.2 all_gather.69
  479.3 18.0 %convert_reduce_fusion.4 = (f32[16,64]{1,0:T(8,128)S(1)}, bf16[16,64,128]{2,1,0:T(8,128)(2,1)}) fusion(bf16[512,16,64]{0,2,1:T(8,128)(2,1)S(1)} %bitcast.122, f32[16,128,512]{2,1,0:T(8,128)} %fusion.73, f32[16,128,512]{2,1,0:T(8,128)} %copy-done, f32[16,128]{1,0:T(8,128)S(1)} %log_add_fusion), kind=kOutput, calls=%fused_computation.60 | convolution fusion | flops 144049664 | bytes 9711616 | tf_op jit(solution)/shard_map/hqk,khd->qhd/dot_general | solution.py:107
  512.4 6.3 fusion.76
  520.0 14.9 %reduce-scatter.3.cloned.1.call-done = f32[128,1024]{0,1:T(8,128)} async-done(((f32[512,1024]{0,1:T(8,128)}), f32[128,1024]{0,1:T(8,128)}) %reduce-scatter.3.cloned.1.call-update) | async-done | bytes 524304 | tf_op jit(solution)/shard_map/reduce_scatter | solution.py:214
  543.4 31.1 %all-gather = f32[49152]{0:T(1024)S(1)} all-gather(f32[6144]{0:T(1024)S(1)} %constant_dynamic-update-slice_fusion), channel_id=2, replica_groups=mesh['rep'=4,'fsdp'=2,'seq'=4] {'fsdp','seq'}, dimensions={0}, use_global_device_ids=true | all-gather | bytes 221184 | tf_op jit(solution)/shard_map/all_gather | solution.py:262
  574.6 8.0 fusion.50
  590.6 8.8 all-reduce.8
  599.7 7.1 convolution_bitcast_fusion
  610.6 62.2 %all-reduce.6 = (f32[3072]{0:T(1024)}, f32[1024]{0:T(1024)}, f32[512]{0:T(512)}, f32[2048]{0:T(1024)}, f32[512]{0:T(512)}) all-reduce(f32[3072]{0:T(1024)S(1)} %dynamic-slice.4, f32[1024]{0:T(1024)S(1)} %dynamic-slice.6, f32[512]{0:T(512)S(1)} %dynamic-slice.8, ...), channel_id=1, replica_groups=mesh['rep'=4,'fsdp'=2,'seq'=4] {'rep','seq'}, use_global_device_ids=true, to_apply=%region_23.24 | all-reduce | flops 7168 | bytes 57344 | tf_op jit(solution)/shard_map/psum | solution.py:279
  673.4 546.8 %all-reduce.11.cloned.1.call-done = (f32[512,6144]{1,0:T(8,128)}, f32[512,3072]{1,0:T(8,128)}, f32[512,1024]{1,0:T(8,128)}, f32[512,4096]{1,0:T(8,128)}, f32[2048,1024]{1,0:T(8,128)}) async-done(((f32[512,6144]{1,0:T(8,128)}, f32[512,3072]{1,0:T(8,128)}, f32[512,1024]{1,0:T(8,128)}, f32[512,4096]{1,0:T(8,128)}, f32[2048,1024]{1,0:T(8,128)}), (f32[512,6144]{1,0:T(8,128)}, f32[512,3072]{1,0:T(8,128)}, ...) | async-done | bytes 37748752 | tf_op jit(solution)/shard_map/psum | solution.py:279
  1220.2 10.8 copy.99
  1231.0 6.9 copy.100
  (165 shorter events, 129.3 us)
Async XLA Ops:
  7.2 31.9 %copy-start.2 = (bf16[1,128,1024]{2,1,0:T(8,128)(2,1)S(1)}, bf16[1,128,1024]{2,1,0:T(8,128)(2,1)}, u32[]{:S(2)}) copy-start(bf16[1,128,1024]{2,1,0:T(8,128)(2,1)} %param.13) | copy-start | bytes 786436
  7.2 86.5 %all-gather.13.cloned.1.call-start = ((), (), s32[]{:S(2)}) async-start(), calls=%async_computation.7 | async-start | bytes 9437184 | tf_op jit(solution)/shard_map/all_gather | solution.py:151
  7.9 118.7 %all-gather.15.cloned.1.call-start = ((), (), s32[]{:S(2)}) async-start(), calls=%async_computation.8 | async-start | bytes 1310720 | tf_op jit(solution)/shard_map/all_gather | solution.py:180
  98.4 57.7 %all-gather.17.cloned.1.call-start = ((), (), s32[]{:S(2)}) async-start(), calls=%async_computation.9 | async-start | bytes 1310720 | tf_op jit(solution)/shard_map/all_gather | solution.py:179
  99.2 90.8 %all-gather.19.cloned.1.call-start = ((), (), s32[]{:S(2)}) async-start(), calls=%async_computation.10 | async-start | bytes 3145728 | tf_op jit(solution)/shard_map/all_gather | solution.py:153
  99.9 195.6 %all-gather.21.cloned.1.call-start = ((), (), s32[]{:S(2)}) async-start(), calls=%async_computation.11 | async-start | bytes 12582912 | tf_op jit(solution)/shard_map/all_gather | solution.py:155
  100.4 300.4 %all-gather.23.cloned.1.call-start = ((), (), s32[]{:S(2)}) async-start(), calls=%async_computation.12 | async-start | bytes 12582912 | tf_op jit(solution)/shard_map/all_gather | solution.py:157
  101.0 411.3 %all-gather.27.cloned.1.call-start = ((), (), s32[]{:S(2)}) async-start(), calls=%async_computation.16 | async-start | bytes 3145728 | tf_op jit(solution)/shard_map/all_gather | solution.py:247
  114.8 286.1 %copy-start.11 = (bf16[128,1024]{1,0:T(8,128)(2,1)}, bf16[128,1024]{1,0:T(8,128)(2,1)S(1)}, u32[]{:S(2)}) copy-start(bf16[128,1024]{1,0:T(8,128)(2,1)S(1)} %get-tuple-element.37) | copy-start | bytes 786436
  115.0 43.6 %copy-start.14 = (bf16[128,1024]{0,1:T(8,128)(2,1)}, bf16[128,1024]{0,1:T(8,128)(2,1)S(1)}, u32[]{:S(2)}) copy-start(bf16[128,1024]{0,1:T(8,128)(2,1)S(1)} %copy.52) | copy-start | bytes 786436
  128.1 31.6 %copy-start.5 = (bf16[512,1024]{0,1:T(8,128)(2,1)}, bf16[512,1024]{0,1:T(8,128)(2,1)S(1)}, u32[]{:S(2)}) copy-start(bf16[512,1024]{0,1:T(8,128)(2,1)S(1)} %copy.51) | copy-start | bytes 3145732
  409.4 109.3 %reduce-scatter.5.cloned.1.call-start = ((), (), s32[]{:S(2)}) async-start(), calls=%async_computation.14 | async-start | bytes 2621440 | tf_op jit(solution)/shard_map/reduce_scatter | solution.py:215
  424.5 110.3 %reduce-scatter.3.cloned.1.call-start = ((), (), s32[]{:S(2)}) async-start(), calls=%async_computation.13 | async-start | bytes 2621440 | tf_op jit(solution)/shard_map/reduce_scatter | solution.py:214
  428.6 19.6 %copy-start.12 = (bf16[128,1024]{1,0:T(8,128)(2,1)S(1)}, bf16[128,1024]{1,0:T(8,128)(2,1)}, u32[]{:S(2)}) copy-start(bf16[128,1024]{1,0:T(8,128)(2,1)} %copy-done.11) | copy-start | bytes 786436
  460.6 14.3 %all-to-all-start.2 = ((bf16[128,2,512]{2,0,1:T(8,128)(2,1)}), bf16[128,2,512]{2,0,1:T(8,128)(2,1)S(1)}, u32[]{:S(2)}, u32[]{:S(2)}) async-start(bf16[128,2,512]{2,0,1:T(8,128)(2,1)} %copy.57), calls=%async_computation.4 | async-start | bytes 524288 | tf_op jit(solution)/shard_map/all_to_all | solution.py:243
  475.7 24.4 %all-to-all-start.4 = ((bf16[128,2,2048]{2,0,1:T(8,128)(2,1)}), bf16[128,2,2048]{2,0,1:T(8,128)(2,1)S(1)}, u32[]{:S(2)}, u32[]{:S(2)}) async-start(bf16[128,2,2048]{2,0,1:T(8,128)(2,1)} %bitcast.114), calls=%async_computation.6 | async-start | bytes 2097152 | tf_op jit(solution)/shard_map/all_to_all | solution.py:242
  479.3 18.0 %copy-start.7 = (bf16[256,1024]{1,0:T(8,128)(2,1)S(1)}, bf16[256,1024]{1,0:T(8,128)(2,1)}, u32[]{:S(2)}) copy-start(bf16[256,1024]{1,0:T(8,128)(2,1)} %all_gather.69) | copy-start | bytes 1572868
  500.0 8.8 all-to-all-start.3
  508.9 73.9 %all-to-all-start.1 = ((bf16[128,2,512]{2,0,1:T(8,128)(2,1)}), bf16[128,2,512]{2,0,1:T(8,128)(2,1)S(1)}, u32[]{:S(2)}, u32[]{:S(2)}) async-start(bf16[128,2,512]{2,0,1:T(8,128)(2,1)} %fusion.42), calls=%async_computation.3 | async-start | bytes 524288 | tf_op jit(solution)/shard_map/all_to_all | solution.py:240
  512.3 70.4 %all-gather.25.cloned.1.call-start = ((), (), s32[]{:S(2)}) async-start(), calls=%async_computation.15 | async-start | bytes 2359296 | tf_op jit(solution)/shard_map/all_gather | solution.py:246
  512.4 23.6 %copy-start.16 = (bf16[16,64,128]{2,1,0:T(8,128)(2,1)S(1)}, bf16[16,64,128]{2,1,0:T(8,128)(2,1)}, u32[]{:S(2)}) copy-start(bf16[16,64,128]{2,1,0:T(8,128)(2,1)} %get-tuple-element.72) | copy-start | bytes 786436
  536.9 683.3 %all-reduce.11.cloned.1.call-start = ((), (), s32[]{:S(2)}) async-start(), calls=%async_computation.17 | async-start | bytes 75497472 | tf_op jit(solution)/shard_map/psum | solution.py:279
  587.9 84.9 %copy-start.17 = (bf16[1,1024]{1,0:T(2,128)(2,1)S(1)}, bf16[1,1024]{1,0:T(2,128)(2,1)}, u32[]{:S(2)}) copy-start(bf16[1,1024]{1,0:T(2,128)(2,1)} %param.14) | copy-start | bytes 6148
  607.3 65.5 %all-to-all-start = ((f32[2,1,512]{2,1,0:T(1,128)}), f32[2,1,512]{2,1,0:T(1,128)S(1)}, u32[]{:S(2)}, u32[]{:S(2)}) async-start(f32[2,1,512]{2,1,0:T(1,128)} %copy.55), calls=%async_computation.2 | async-start | bytes 8192 | tf_op jit(solution)/shard_map/all_to_all | solution.py:277
  (15 other events, 85.9 us)
Sparse Core Ops, SparseCore 0:
  9.5 84.1 all-gather.12
  98.5 28.0 all-gather.14
  128.8 27.3 all-gather.16
  157.6 32.4 all-gather.18
  191.4 103.9 all-gather.20
  296.9 103.9 all-gather.22
  409.5 33.0 all-gather.26
  445.5 43.6 reduce-scatter.4
  492.0 42.8 reduce-scatter.2
  537.0 27.5 all-gather.24
  588.0 632.1 all-reduce.10
where the time goes:
time: 1260 us
  waiting for transfers between devices  885 us (70%)
  blocking collectives  157 us (12%)
  matrix products  124 us (10%)
  local copies, waits for them, and re-layouts  43 us (3%)
  starting transfers between devices  18 us (1%)
  between operations  17.2 us (1%)
    psum x1, waiting for transfers between devices, local(): lax.psum((ada_shard, adab_shard, qkv_shard, qv_shard, proj_shard, projb_s...  547 us
    all_gather x1, waiting for transfers between devices, local(): lax.all_gather(fc1_weight, 'fsdp', axis=0, tiled=True)  101 us
    all_gather x1, waiting for transfers between devices, local(): lax.all_gather(fc2_weight, 'fsdp', axis=0, tiled=True)  98.7 us
    psum x1, blocking collectives, local(): lax.psum((ada_shard, adab_shard, qkv_shard, qv_shard, proj_shard, projb_s...  62.2 us
    all_gather x1, waiting for transfers between devices, local(): lax.all_gather(qkv_weight, 'fsdp', axis=0, tiled=True)  53.5 us
    unnamed x65, local copies, waits for them, and re-layouts  32.3 us
    all_gather x1, blocking collectives, local(): lax.all_gather(mods_grad[None, :], ('fsdp', 'seq'), axis=0, tiled=True)  31.1 us
    all_gather x1, waiting for transfers between devices, local(): lax.all_gather(key_rows, 'seq', axis=0, tiled=True)  28 us
  transfers between devices with their start and end apart: 16, of which 9 were waited for; matrix products, arithmetic and copies ran while one was open for 10% of the time, Pallas kernels for 0%

commit v1 on v0

--- a/solution.py
+++ b/solution.py
@@ -277,19 +277,22 @@
     cond_sum = lax.all_to_all(cond_part, "fsdp", split_axis=0, concat_axis=1, tiled=True)
     cond_grad = cond_sum * silu_slope(cond_f)
     sums = lax.psum(
-        (
-            ada_shard,
-            adab_shard,
-            qkv_shard,
-            qv_shard,
-            proj_shard,
-            projb_shard,
-            fc1_shard,
-            fc1b_shard,
-            fc2_shard,
-            fc2b_shard,
+        lax.psum(
+            (
+                ada_shard,
+                adab_shard,
+                qkv_shard,
+                qv_shard,
+                proj_shard,
+                projb_shard,
+                fc1_shard,
+                fc1b_shard,
+                fc2_shard,
+                fc2b_shard,
+            ),
+            "seq",
         ),
-        ("rep", "seq"),
+        "rep",
     )
     return (
         output[None],

time: 1260 us -> 2500 us (1.98)
  waiting for transfers between devices: 885 us -> 2150 us
  blocking collectives: 157 us -> 124 us
    psum x1, waiting for transfers between devices: 547 us -> 1240 us  [local(): lax.psum((ada_shard, adab_shard, qkv_shard, qv_shard, proj_shard, projb_s...]
    psum x0 -> x1, waiting for transfers between devices: none -> 577 us  [local(): lax.psum(lax.psum((ada_shard, adab_shard, qkv_shard, qv_shard, proj_shard...]
    psum x1, blocking collectives: 62.2 us -> 15.9 us  [local(): lax.psum((ada_shard, adab_shard, qkv_shard, qv_shard, proj_shard, projb_s...]
  transfers between devices with their start and end apart: 16 -> 17, of which waited for: 9 -> 10; matrix products, arithmetic and copies ran while one was open for 10% -> 5% of each run, Pallas kernels for 0% -> 0%
where the time goes in v1:
time: 2500 us; the launch traced here: 2490 us
  waiting for transfers between devices  2150 us (86%)
  blocking collectives  124 us (5%)
  matrix products  123 us (5%)
  local copies, waits for them, and re-layouts  43 us (2%)
    psum x1, waiting for transfers between devices, local(): lax.psum((ada_shard, adab_shard, qkv_shard, qv_shard, proj_shard, projb_s...  1240 us
    psum x1, waiting for transfers between devices, local(): lax.psum(lax.psum((ada_shard, adab_shard, qkv_shard, qv_shard, proj_shard...  577 us
    all_gather x1, waiting for transfers between devices, local(): lax.all_gather(fc1_weight, 'fsdp', axis=0, tiled=True)  101 us
    all_gather x1, waiting for transfers between devices, local(): lax.all_gather(fc2_weight, 'fsdp', axis=0, tiled=True)  98.7 us
    all_gather x1, waiting for transfers between devices, local(): lax.all_gather(qkv_weight, 'fsdp', axis=0, tiled=True)  53.5 us
  transfers between devices with their start and end apart: 17, of which 10 were waited for; matrix products, arithmetic and copies ran while one was open for 5% of the time, Pallas kernels for 0%

profile of v1, /device:TPU:0, one launch (start us, length us, event | category | flops | bytes accessed | tf_op | source)
XLA Modules:
  0.0 2491.4 jit_solution(13890675977704296122)
XLA Ops:
  28.7 10.4 all-reduce
  40.2 53.5 %all-gather.13.cloned.1.call-done = bf16[1024,3072]{1,0:T(8,128)(2,1)} async-done(((bf16[512,3072]{1,0:T(8,128)(2,1)}), bf16[1024,3072]{1,0:T(8,128)(2,1)}) %all-gather.13.cloned.1.call-update) | async-done | bytes 6291472 | tf_op jit(solution)/shard_map/all_gather | solution.py:151
  115.0 11.7 all-gather.15.cloned.1.call-done
  128.1 28.0 %all-gather.17.cloned.1.call-done = bf16[512,1024]{1,0:T(8,128)(2,1)} async-done(((bf16[128,1024]{1,0:T(8,128)(2,1)}), bf16[512,1024]{1,0:T(8,128)(2,1)}) %all-gather.17.cloned.1.call-update) | async-done | bytes 1048592 | tf_op jit(solution)/shard_map/all_gather | solution.py:179
  162.7 27.4 %all-gather.19.cloned.1.call-done = bf16[1024,1024]{1,0:T(8,128)(2,1)} async-done(((bf16[512,1024]{1,0:T(8,128)(2,1)}), bf16[1024,1024]{1,0:T(8,128)(2,1)}) %all-gather.19.cloned.1.call-update) | async-done | bytes 2097168 | tf_op jit(solution)/shard_map/all_gather | solution.py:153
  194.1 101.3 %all-gather.21.cloned.1.call-done = bf16[1024,4096]{1,0:T(8,128)(2,1)} async-done(((bf16[512,4096]{1,0:T(8,128)(2,1)}), bf16[1024,4096]{1,0:T(8,128)(2,1)}) %all-gather.21.cloned.1.call-update) | async-done | bytes 8388624 | tf_op jit(solution)/shard_map/all_gather | solution.py:155
  302.1 98.7 %all-gather.23.cloned.1.call-done = bf16[4096,1024]{1,0:T(8,128)(2,1)} async-done(((bf16[2048,1024]{1,0:T(8,128)(2,1)}), bf16[4096,1024]{1,0:T(8,128)(2,1)}) %all-gather.23.cloned.1.call-update) | async-done | bytes 8388624 | tf_op jit(solution)/shard_map/all_gather | solution.py:157
  400.9 8.5 convert_reduce_fusion
  409.6 6.9 multiply_reduce_fusion.2
  428.6 18.3 fusion.8
  448.2 8.5 all_gather.71
  466.8 8.2 all_gather.69
  479.3 18.0 convert_reduce_fusion.4
  519.9 15.0 reduce-scatter.3.cloned.1.call-done
  543.4 31.1 %all-gather = f32[49152]{0:T(1024)S(1)} all-gather(f32[6144]{0:T(1024)S(1)} %constant_dynamic-update-slice_fusion), channel_id=2, replica_groups=mesh['rep'=4,'fsdp'=2,'seq'=4] {'fsdp','seq'}, dimensions={0}, use_global_device_ids=true | all-gather | bytes 221184 | tf_op jit(solution)/shard_map/all_gather | solution.py:262
  574.7 8.1 fusion.50
  587.9 1239.0 %all-reduce.14.cloned.1.call-done = (f32[512,6144]{1,0:T(8,128)}, f32[512,3072]{1,0:T(8,128)}, f32[512,1024]{1,0:T(8,128)}, f32[512,4096]{1,0:T(8,128)}, f32[2048,1024]{1,0:T(8,128)}) async-done(((f32[512,6144]{1,0:T(8,128)}, f32[512,3072]{1,0:T(8,128)}, f32[512,1024]{1,0:T(8,128)}, f32[512,4096]{1,0:T(8,128)}, f32[2048,1024]{1,0:T(8,128)}), (f32[512,6144]{1,0:T(8,128)}, f32[512,3072]{1,0:T(8,128)}, ...) | async-done | bytes 37748752 | tf_op jit(solution)/shard_map/psum | solution.py:280
  1829.6 8.8 all-reduce.10
  1838.7 7.0 convolution_bitcast_fusion
  1849.6 15.9 all-reduce.6
  1865.5 12.8 all-reduce.8
  1878.9 576.8 %all-reduce.16.cloned.1.call-done = (f32[512,6144]{1,0:T(8,128)}, f32[512,3072]{1,0:T(8,128)}, f32[512,1024]{1,0:T(8,128)}, f32[512,4096]{1,0:T(8,128)}, f32[2048,1024]{1,0:T(8,128)}) async-done(((f32[512,6144]{1,0:T(8,128)}, f32[512,3072]{1,0:T(8,128)}, f32[512,1024]{1,0:T(8,128)}, f32[512,4096]{1,0:T(8,128)}, f32[2048,1024]{1,0:T(8,128)}), (f32[512,6144]{1,0:T(8,128)}, f32[512,3072]{1,0:T(8,128)}, ...) | async-done | bytes 37748752 | tf_op jit(solution)/shard_map/psum | solution.py:279
  2455.7 10.8 copy.104
  2466.6 6.9 copy.105
  (169 shorter events, 142.4 us)
Async XLA Ops:
  7.2 31.9 %copy-start.2 = (bf16[1,128,1024]{2,1,0:T(8,128)(2,1)S(1)}, bf16[1,128,1024]{2,1,0:T(8,128)(2,1)}, u32[]{:S(2)}) copy-start(bf16[1,128,1024]{2,1,0:T(8,128)(2,1)} %param.13) | copy-start | bytes 786436
  7.2 86.5 %all-gather.13.cloned.1.call-start = ((), (), s32[]{:S(2)}) async-start(), calls=%async_computation.7 | async-start | bytes 9437184 | tf_op jit(solution)/shard_map/all_gather | solution.py:151
  7.9 118.7 %all-gather.15.cloned.1.call-start = ((), (), s32[]{:S(2)}) async-start(), calls=%async_computation.8 | async-start | bytes 1310720 | tf_op jit(solution)/shard_map/all_gather | solution.py:180
  98.4 57.7 %all-gather.17.cloned.1.call-start = ((), (), s32[]{:S(2)}) async-start(), calls=%async_computation.9 | async-start | bytes 1310720 | tf_op jit(solution)/shard_map/all_gather | solution.py:179
  99.2 90.8 %all-gather.19.cloned.1.call-start = ((), (), s32[]{:S(2)}) async-start(), calls=%async_computation.10 | async-start | bytes 3145728 | tf_op jit(solution)/shard_map/all_gather | solution.py:153
  99.9 195.6 %all-gather.21.cloned.1.call-start = ((), (), s32[]{:S(2)}) async-start(), calls=%async_computation.11 | async-start | bytes 12582912 | tf_op jit(solution)/shard_map/all_gather | solution.py:155
  100.4 300.4 %all-gather.23.cloned.1.call-start = ((), (), s32[]{:S(2)}) async-start(), calls=%async_computation.12 | async-start | bytes 12582912 | tf_op jit(solution)/shard_map/all_gather | solution.py:157
  101.0 411.3 %all-gather.27.cloned.1.call-start = ((), (), s32[]{:S(2)}) async-start(), calls=%async_computation.16 | async-start | bytes 3145728 | tf_op jit(solution)/shard_map/all_gather | solution.py:247
  114.8 286.1 %copy-start.11 = (bf16[128,1024]{1,0:T(8,128)(2,1)}, bf16[128,1024]{1,0:T(8,128)(2,1)S(1)}, u32[]{:S(2)}) copy-start(bf16[128,1024]{1,0:T(8,128)(2,1)S(1)} %get-tuple-element.47) | copy-start | bytes 786436
  115.0 43.6 %copy-start.14 = (bf16[128,1024]{0,1:T(8,128)(2,1)}, bf16[128,1024]{0,1:T(8,128)(2,1)S(1)}, u32[]{:S(2)}) copy-start(bf16[128,1024]{0,1:T(8,128)(2,1)S(1)} %copy.52) | copy-start | bytes 786436
  128.1 31.6 %copy-start.5 = (bf16[512,1024]{0,1:T(8,128)(2,1)}, bf16[512,1024]{0,1:T(8,128)(2,1)S(1)}, u32[]{:S(2)}) copy-start(bf16[512,1024]{0,1:T(8,128)(2,1)S(1)} %copy.51) | copy-start | bytes 3145732
  409.4 109.3 %reduce-scatter.5.cloned.1.call-start = ((), (), s32[]{:S(2)}) async-start(), calls=%async_computation.14 | async-start | bytes 2621440 | tf_op jit(solution)/shard_map/reduce_scatter | solution.py:215
  424.5 110.4 %reduce-scatter.3.cloned.1.call-start = ((), (), s32[]{:S(2)}) async-start(), calls=%async_computation.13 | async-start | bytes 2621440 | tf_op jit(solution)/shard_map/reduce_scatter | solution.py:214
  428.6 19.6 copy-start.12
  460.6 14.3 all-to-all-start.2
  475.7 24.3 all-to-all-start.4
  500.0 8.8 all-to-all-start.3
  508.8 73.9 %all-to-all-start.1 = ((bf16[128,2,512]{2,0,1:T(8,128)(2,1)}), bf16[128,2,512]{2,0,1:T(8,128)(2,1)S(1)}, u32[]{:S(2)}, u32[]{:S(2)}) async-start(bf16[128,2,512]{2,0,1:T(8,128)(2,1)} %fusion.42), calls=%async_computation.3 | async-start | bytes 524288 | tf_op jit(solution)/shard_map/all_to_all | solution.py:240
  512.3 70.5 %all-gather.25.cloned.1.call-start = ((), (), s32[]{:S(2)}) async-start(), calls=%async_computation.15 | async-start | bytes 2359296 | tf_op jit(solution)/shard_map/all_gather | solution.py:246
  512.3 23.6 copy-start.16
  537.0 1290.0 %all-reduce.14.cloned.1.call-start = ((), (), s32[]{:S(2)}) async-start(), calls=%async_computation.17 | async-start | bytes 75497472 | tf_op jit(solution)/shard_map/psum | solution.py:280
  587.9 1867.8 %all-reduce.16.cloned.1.call-start = ((), (), s32[]{:S(2)}) async-start(), calls=%async_computation.18 | async-start | bytes 75497472 | tf_op jit(solution)/shard_map/psum | solution.py:279
  1826.9 51.4 %copy-start.17 = (bf16[1,1024]{1,0:T(2,128)(2,1)S(1)}, bf16[1,1024]{1,0:T(2,128)(2,1)}, u32[]{:S(2)}) copy-start(bf16[1,1024]{1,0:T(2,128)(2,1)} %param.14) | copy-start | bytes 6148
  1846.3 32.0 %all-to-all-start = ((f32[2,1,512]{2,1,0:T(1,128)}), f32[2,1,512]{2,1,0:T(1,128)S(1)}, u32[]{:S(2)}, u32[]{:S(2)}) async-start(f32[2,1,512]{2,1,0:T(1,128)} %copy.55), calls=%async_computation.2 | async-start | bytes 8192 | tf_op jit(solution)/shard_map/all_to_all | solution.py:277
  (16 other events, 103.9 us)
Sparse Core Ops, SparseCore 0:
  9.5 84.1 all-gather.12
  98.5 28.0 all-gather.14
  128.8 27.3 all-gather.16
  157.6 32.4 all-gather.18
  191.4 103.9 all-gather.20
  296.9 103.9 all-gather.22
  409.5 33.0 all-gather.26
  445.5 43.6 reduce-scatter.4
  492.0 42.8 reduce-scatter.2
  537.1 27.5 all-gather.24
  588.0 1238.8 all-reduce.13
  1829.8 625.8 all-reduce.15
